TPU v7x, 512 devices: a whole 4x8x8 slice. The times are simulated.
512 devices in a mesh: wide: 64 (over y, z), narrow: 8 (over x, core).
Axes of the slice: x: 4, y: 8, z: 8, core: 2. Of those that a mesh axis runs over, the one named last changes fastest.
Arguments:
- hidden: bfloat16 [16384, 1536], P('wide', 'narrow'), may hold values from -6 to 6
- start_state: bfloat16 [1024, 24, 64, 128], P('wide', 'narrow'), may hold values from -0.59765625 to 0.59765625
- tail_inner: bfloat16 [1024, 3, 1536], P('wide', None, 'narrow'), may hold values from -6 to 6
- tail_shared: bfloat16 [1024, 3, 256], P('wide'), may hold values from -6 to 6
- input_gain: float32 [1536], replicated, may hold values from 0.5 to 1.5
- w_gate_inner: bfloat16 [1536, 3072], P(None, 'narrow'), may hold values from -0.15625 to 0.15625
- w_shared: bfloat16 [1536, 256], P(None, 'narrow'), may hold values from -0.15625 to 0.15625
- w_step: bfloat16 [1536, 24], P(None, 'narrow'), may hold values from -0.15625 to 0.15625
- step_bias: float32 [24], P('narrow'), may hold values from -4 to -1
- decay_log: float32 [24], P('narrow'), may hold values from 0 to 2.5
- conv_inner: bfloat16 [4, 1536], P(None, 'narrow'), may hold values from -3 to 3
- conv_inner_bias: float32 [1536], P('narrow'), may hold values from -1.5 to 1.5
- conv_shared: bfloat16 [4, 256], replicated, may hold values from -3 to 3
- conv_shared_bias: float32 [256], replicated, may hold values from -1.5 to 1.5
- skip_gain: float32 [24], P('narrow'), may hold values from 0.5 to 1.5
- gated_gain: float32 [1536], P('narrow'), may hold values from 0.5 to 1.5
- w_output: bfloat16 [1536, 1536], P('narrow'), may hold values from -0.15625 to 0.15625
- next_gain: float32 [1536], replicated, may hold values from 0.5 to 1.5
- w_next: bfloat16 [1536, 3224], P(None, 'narrow'), may hold values from -0.15625 to 0.15625
- dealing: int32 [1024], replicated, may hold values from 0 to 1023, as said below
- accepted: int32 [1024], replicated, may hold values from 0 to 16
- owners: int32 [1024], replicated, may hold values from 0 to 63, as said below
Outputs:
- new_hidden: bfloat16 [16384, 1536], P('wide', 'narrow')
- next_input: bfloat16 [16384, 3224], P('wide', 'narrow')
- kept_state: bfloat16 [1024, 24, 64, 128], P('wide', 'narrow')
- kept_tail_inner: bfloat16 [1024, 3, 1536], P('wide', None, 'narrow')
- kept_tail_shared: bfloat16 [1024, 3, 256], P('wide')
Inputs may be any that keep to these rules, and one draw needn't show every extreme that they name: `dealing`: a permutation of the 1024 requests; slot j lies on index j // 16 of wide. Each owner keeps exactly 16 requests, and the requests of the slots of one index of wide have different owners.
All inputs are finite; a program needn't handle non-finite values.
Results may differ from a plain program's by a relative error of at most 0.02.
Values may be sent and summed in bfloat16 or wider, within the bound.
A program may use at most 64 MiB of HBM per device.

v0:
```python
import jax
import jax.numpy as jnp
from jax import lax
from jax.sharding import PartitionSpec as P

EPSILON = 1e-05
HIGHEST = lax.Precision.HIGHEST


def root_norm(values, gain):
    values = values.astype(jnp.float32)
    factor = lax.rsqrt(jnp.mean(values * values, axis=-1, keepdims=True) + EPSILON)
    return (values * factor * gain).astype(jnp.bfloat16)


def causal_filter(tail, fresh, weight, offset):
    extended = jnp.concatenate([tail, fresh], axis=1)
    length = fresh.shape[1]
    summed = jnp.zeros(fresh.shape, jnp.float32) + offset
    for place in range(weight.shape[0]):
        summed = summed + extended[:, place : place + length].astype(jnp.float32) * weight[
            place
        ].astype(jnp.float32)
    return (jax.nn.silu(summed), extended)


def pick_rows(extended, accepted_now, count):
    length = extended.shape[1]
    wanted = accepted_now[:, None] + jnp.arange(count, dtype=jnp.int32)[None, :]
    onehot = (wanted[:, :, None] == jnp.arange(length, dtype=jnp.int32)[None, None, :]).astype(
        jnp.float32
    )
    return jnp.einsum(
        "rqe,rec->rqc", onehot, extended.astype(jnp.float32), precision=HIGHEST
    ).astype(jnp.bfloat16)


def state_block(
    inner, shared, step_raw, step_bias, decay_log, skip_gain, start_state, accepted_now
):
    states = shared.shape[-1] // 2
    b_part = shared[..., :states]
    c_part = shared[..., states:]
    length = inner.shape[1]
    steps_now = jax.nn.softplus(step_raw.astype(jnp.float32) + step_bias)
    log_decay = steps_now * -jnp.exp(decay_log)
    cumul = jnp.cumsum(log_decay, axis=1)
    prefix = jnp.concatenate([jnp.zeros_like(cumul[:, :1]), cumul], axis=1)
    places = jnp.arange(length, dtype=jnp.int32)
    lower = (places[:, None] >= places[None, :])[None, :, :, None]
    spread = cumul[:, :, None, :] - cumul[:, None, :, :]
    weights = (
        jnp.where(lower, jnp.exp(jnp.where(lower, spread, 0.0)), 0.0) * steps_now[:, None, :, :]
    )
    intersection = jnp.einsum("rtn,rsn->rts", c_part, b_part, precision=HIGHEST)
    mixing = weights * intersection[:, :, :, None]
    state_now = start_state.astype(jnp.float32)
    carried = (
        jnp.einsum("rtn,rhpn->rthp", c_part, state_now, precision=HIGHEST)
        * jnp.exp(cumul)[:, :, :, None]
    )
    direct = jnp.einsum("rtsh,rshp->rthp", mixing, inner, precision=HIGHEST)
    outputs = carried + direct + skip_gain[:, None] * inner
    chosen = (jnp.arange(length + 1, dtype=jnp.int32)[None, :] == accepted_now[:, None]).astype(
        jnp.float32
    )
    ending = jnp.einsum("rk,rkh->rh", chosen, prefix, precision=HIGHEST)
    before = (places[None, :] < accepted_now[:, None])[:, :, None]
    factor = (
        jnp.where(before, jnp.exp(jnp.where(before, ending[:, None, :] - cumul, 0.0)), 0.0)
        * steps_now
    )
    kept = jnp.exp(ending)[:, :, None, None] * state_now + jnp.einsum(
        "rsh,rshp,rsn->rhpn", factor, inner, b_part, precision=HIGHEST
    )
    return (outputs, kept.astype(jnp.bfloat16))


def local(
    hidden,
    start_state,
    tail_inner,
    tail_shared,
    input_gain,
    w_gate_inner,
    w_shared,
    w_step,
    step_bias,
    decay_log,
    conv_inner,
    conv_inner_bias,
    conv_shared,
    conv_shared_bias,
    skip_gain,
    gated_gain,
    w_output,
    next_gain,
    w_next,
    dealing,
    accepted,
    owners,
):
    wide_index = lax.axis_index("wide")
    wide_count = lax.axis_size("wide")
    narrow_count = lax.axis_size("narrow")
    full_rows = lax.all_gather(hidden, "narrow", axis=1, tiled=True)
    normed_in = root_norm(full_rows, input_gain)
    tokens = full_rows.shape[0]
    requests = start_state.shape[0]
    length = tokens // requests
    heads_here = w_step.shape[1]
    head_size = start_state.shape[2]
    block = w_output.shape[0]
    gate_inner = jnp.dot(normed_in, w_gate_inner, preferred_element_type=jnp.float32).astype(
        jnp.bfloat16
    )
    shared_piece = jnp.dot(normed_in, w_shared, preferred_element_type=jnp.float32).astype(
        jnp.bfloat16
    )
    step_raw = jnp.dot(normed_in, w_step, preferred_element_type=jnp.float32).astype(jnp.bfloat16)
    shared_in = lax.all_gather(shared_piece, "narrow", axis=1, tiled=True)
    gate_part = gate_inner[:, :block]
    inner_in = gate_inner[:, block:]
    inner_conv, inner_ext = causal_filter(
        tail_inner, inner_in.reshape(requests, length, block), conv_inner, conv_inner_bias
    )
    shared_conv, shared_ext = causal_filter(
        tail_shared, shared_in.reshape(requests, length, -1), conv_shared, conv_shared_bias
    )
    first_slot = wide_index * requests
    slot_requests = lax.dynamic_slice_in_dim(dealing, first_slot, requests)
    accepted_now = jnp.take(accepted, slot_requests)
    outputs, kept = state_block(
        inner_conv.reshape(requests, length, heads_here, head_size),
        shared_conv,
        step_raw.reshape(requests, length, heads_here),
        step_bias,
        decay_log,
        skip_gain,
        start_state,
        accepted_now,
    )
    gated = outputs.reshape(tokens, block) * jax.nn.silu(gate_part.astype(jnp.float32))
    squares = lax.psum(jnp.sum(gated * gated, axis=1, keepdims=True), "narrow")
    gated_norm = (
        gated * lax.rsqrt(squares / (block * narrow_count) + EPSILON) * gated_gain
    ).astype(jnp.bfloat16)
    partial_sum = jnp.dot(gated_norm, w_output, preferred_element_type=jnp.float32)
    whole_sum = lax.psum(partial_sum.astype(jnp.bfloat16), "narrow").astype(jnp.float32)
    new_full = (full_rows.astype(jnp.float32) + whole_sum).astype(jnp.bfloat16)
    new_part = lax.dynamic_slice_in_dim(
        new_full, lax.axis_index("narrow") * hidden.shape[1], hidden.shape[1], 1
    )
    normed_next = root_norm(new_full, next_gain)
    next_input = jnp.dot(normed_next, w_next, preferred_element_type=jnp.float32).astype(
        jnp.bfloat16
    )
    owner_table = (owners[:, None] == jnp.arange(wide_count, dtype=jnp.int32)[None, :]).astype(
        jnp.int32
    )
    ranking = jnp.sum((jnp.cumsum(owner_table, axis=0) - owner_table) * owner_table, axis=1)
    slot_owner = jnp.take(owners, dealing)
    slot_rank = jnp.take(ranking, dealing)
    local_owner = lax.dynamic_slice_in_dim(slot_owner, first_slot, requests)
    send_table = (jnp.arange(wide_count, dtype=jnp.int32)[:, None] == local_owner[None, :]).astype(
        jnp.bfloat16
    )
    state_bucket = (
        jnp.dot(send_table, kept.reshape(requests, -1), preferred_element_type=jnp.float32)
        .astype(jnp.bfloat16)
        .reshape((wide_count,) + kept.shape[1:])
    )
    inner_edge = pick_rows(inner_ext, accepted_now, tail_inner.shape[1])
    shared_edge = pick_rows(shared_ext, accepted_now, tail_shared.shape[1])
    inner_bucket = jnp.einsum(
        "or,rqc->oqc", send_table, inner_edge, preferred_element_type=jnp.float32
    ).astype(jnp.bfloat16)
    shared_bucket = jnp.einsum(
        "or,rqc->oqc", send_table, shared_edge, preferred_element_type=jnp.float32
    ).astype(jnp.bfloat16)
    state_recv, inner_recv, shared_recv = (
        lax.all_to_all(state_bucket, "wide", split_axis=0, concat_axis=0, tiled=True),
        lax.all_to_all(inner_bucket, "wide", split_axis=0, concat_axis=0, tiled=True),
        lax.all_to_all(shared_bucket, "wide", split_axis=0, concat_axis=0, tiled=True),
    )
    senders = jnp.arange(slot_owner.shape[0], dtype=jnp.int32) // requests
    mine = slot_owner == wide_index
    picking = (
        (slot_rank[:, None] == jnp.arange(requests, dtype=jnp.int32)[None, :]) & mine[:, None]
    ).astype(jnp.bfloat16)
    from_sender = (senders[:, None] == jnp.arange(wide_count, dtype=jnp.int32)[None, :]).astype(
        jnp.bfloat16
    )
    selector = jnp.einsum(
        "jk,jw->kw", picking, from_sender, preferred_element_type=jnp.float32
    ).astype(jnp.bfloat16)
    kept_state = (
        jnp.dot(selector, state_recv.reshape(wide_count, -1), preferred_element_type=jnp.float32)
        .astype(jnp.bfloat16)
        .reshape(start_state.shape)
    )
    kept_tail_inner = jnp.einsum(
        "kw,wqc->kqc", selector, inner_recv, preferred_element_type=jnp.float32
    ).astype(jnp.bfloat16)
    kept_tail_shared = jnp.einsum(
        "kw,wqc->kqc", selector, shared_recv, preferred_element_type=jnp.float32
    ).astype(jnp.bfloat16)
    return (new_part, next_input, kept_state, kept_tail_inner, kept_tail_shared)


def solution(mesh):
    placed = (
        P("wide", "narrow"),
        P("wide", "narrow", None, None),
        P("wide", None, "narrow"),
        P("wide", None, None),
        P(),
        P(None, "narrow"),
        P(None, "narrow"),
        P(None, "narrow"),
        P("narrow"),
        P("narrow"),
        P(None, "narrow"),
        P("narrow"),
        P(),
        P(),
        P("narrow"),
        P("narrow"),
        P("narrow", None),
        P(),
        P(None, "narrow"),
        P(),
        P(),
        P(),
    )
    return jax.shard_map(
        local,
        mesh=mesh,
        in_specs=placed,
        out_specs=(
            P("wide", "narrow"),
            P("wide", "narrow"),
            P("wide", "narrow", None, None),
            P("wide", None, "narrow"),
            P("wide", None, None),
        ),
        check_vma=False,
    )
```

profile of v0, /device:TPU:24, one launch (start us, length us, event | category | flops | bytes accessed | tf_op | source)
XLA Modules:
  0.0 219.7 jit_solution(16669502044702229559)
XLA Ops:
  7.2 0.8 fusion.81
  8.0 0.8 compare_select_fusion.2
  8.8 1.3 gather_fusion
  10.1 0.8 and_select_fusion
  10.9 4.5 %gather_fusion.2 = s32[1024]{0:T(1024)S(1)} fusion(s32[1024]{0:T(1024)S(1)} %copy-done.1, s32[1024]{0:T(1024)S(1)} %fusion.81), kind=kCustom, calls=%fused_computation.1.clone | custom fusion | bytes 12288 | tf_op jit(solution)/shard_map/jit(_take)/gather | solution.py:162
  15.4 0.6 broadcast_compare_fusion
  16.2 13.7 %all_gather.6 = bf16[256,1536]{0,1:T(8,128)(2,1)S(1)} all-gather(bf16[256,192]{0,1:T(8,128)(2,1)S(1)} %copy-done.7), channel_id=1, replica_groups=mesh['wide'=64,'narrow'=8] {'narrow'}, dimensions={1}, use_global_device_ids=true | all-gather | bytes 884736 | tf_op jit(solution)/shard_map/all_gather | solution.py:106
  30.5 1.9 convolution_convert_fusion.4
  32.6 0.5 copy-done.6
  33.7 0.7 copy.98
  34.4 16.6 %all-to-all-start.1 = ((bf16[64,3,192]{2,1,0:T(4,128)(2,1)}), bf16[64,3,192]{2,1,0:T(4,128)(2,1)}, u32[]{:S(2)}, u32[]{:S(2)}) async-start(bf16[64,3,192]{2,1,0:T(4,128)(2,1)} %copy.98), calls=%async_computation.1 | async-start | bytes 262144 | tf_op jit(solution)/shard_map/all_to_all | solution.py:183
  51.2 0.6 slice_convert_fusion.7
  51.9 0.4 fusion.15
  52.3 0.4 convolution_convert_fusion.11
  53.1 0.7 fusion.90
  54.4 0.8 copy.95
  55.2 12.7 %all_gather.7 = bf16[256,256]{0,1:T(8,128)(2,1)S(1)} all-gather(bf16[256,32]{0,1:T(8,128)(2,1)S(1)} %convolution_convert_fusion.11), channel_id=1, replica_groups=mesh['wide'=64,'narrow'=8] {'narrow'}, dimensions={1}, use_global_device_ids=true | all-gather | bytes 147456 | tf_op jit(solution)/shard_map/all_gather | solution.py:121
  68.7 0.7 copy.101
  69.4 0.9 divide_multiply_fusion
  70.4 1.1 reshape.238
  71.5 2.2 %broadcast_multiply_fusion = f32[16,16,3,64]{3,2,1,0:T(4,128)} fusion(f32[16,16,3,64]{3,2,1,0:T(4,128)S(1)} %reshape.238, f32[16,16,3]{2,1,0:T(8,128)} %copy.95), kind=kLoop, calls=%fused_computation.72 | loop fusion | flops 49152 | bytes 396288 | tf_op jit(solution)/shard_map/rsh,rshp,rsn->rhpn/dot_general | solution.py:73
  73.7 1.5 divide_multiply_fusion.1
  75.2 12.7 %all-to-all-start.2 = ((bf16[64,3,256]{2,1,0:T(4,128)(2,1)}), bf16[64,3,256]{2,1,0:T(4,128)(2,1)S(1)}, u32[]{:S(2)}, u32[]{:S(2)}) async-start(bf16[64,3,256]{2,1,0:T(4,128)(2,1)} %copy.101), calls=%async_computation.2 | async-start | bytes 262144 | tf_op jit(solution)/shard_map/all_to_all | solution.py:184
  87.9 3.8 %add_convert_fusion = bf16[16,3,64,128]{3,2,1,0:T(8,128)(2,1)S(1)} fusion(bf16[16,3,64,128]{3,2,1,0:T(8,128)(2,1)S(1)} %copy-done.2, f32[16,3]{1,0:T(8,128)S(1)} %copy.93, f32[16,16,3,64]{3,2,1,0:T(4,128)} %broadcast_multiply_fusion, f32[16,16,256]{2,1,0:T(8,128)S(1)} %divide_multiply_fusion.1), kind=kOutput, calls=%fused_computation.21 | convolution fusion | flops 77070336 | bytes 1908736 | tf_op jit(solution)/shard_map/rsh,rshp,rsn->rhpn/dot_general | solution.py:73
  91.7 1.8 fusion.2
  93.5 2.5 %copy.114 = bf16[8,8,192,128]{3,2,1,0:T(8,128)(2,1)} copy(bf16[8,8,192,128]{3,1,2,0:T(8,128)(2,1)S(1)} %fusion.2) | data formatting | bytes 6291456
  96.0 2.8 %all-to-all-done.2 = bf16[64,3,256]{2,1,0:T(4,128)(2,1)S(1)} async-done(((bf16[64,3,256]{2,1,0:T(4,128)(2,1)}), bf16[64,3,256]{2,1,0:T(4,128)(2,1)S(1)}, u32[]{:S(2)}, u32[]{:S(2)}) %all-to-all-start.2) | async-done | bytes 98336 | tf_op jit(solution)/shard_map/all_to_all | solution.py:184
  98.8 10.3 %all-to-all-start = ((bf16[64,3,64,128]{3,2,1,0:T(8,128)(2,1)}), bf16[64,3,64,128]{3,2,1,0:T(8,128)(2,1)}, u32[]{:S(2)}, u32[]{:S(2)}) async-start(bf16[64,3,64,128]{3,2,1,0:T(8,128)(2,1)} %bitcast.87), calls=%async_computation | async-start | bytes 6291456 | tf_op jit(solution)/shard_map/all_to_all | solution.py:182
  109.1 0.6 copy.87
  109.7 0.8 copy.85
  110.8 0.3 fusion.59
  111.1 1.7 convolution_multiply_fusion
  112.9 0.6 fusion.14
  113.7 0.3 reshape.239
  114.0 1.1 multiply_reduce_fusion
  115.1 14.5 %psum.14 = f32[256,1]{0,1:T(1,128)S(1)} all-reduce(f32[256,1]{0,1:T(1,128)S(1)} %bitcast.96), channel_id=1, replica_groups=mesh['wide'=64,'narrow'=8] {'narrow'}, use_global_device_ids=true, to_apply=%region_3.4 | all-reduce | flops 256 | bytes 2048 | tf_op jit(solution)/shard_map/psum | solution.py:144
  129.7 2.4 %convolution_convert_fusion.2 = bf16[256,1536]{1,0:T(8,128)(2,1)} fusion(bf16[192,1536]{1,0:T(8,128)(2,1)} %param.40, f32[192]{0:T(256)S(1)} %copy-done.24, f32[256]{0:T(256)S(1)} %bitcast.105, f32[256,192]{1,0:T(8,128)S(1)} %reshape.239, bf16[256,384]{1,0:T(8,128)(2,1)} %copy-done.6), kind=kOutput, calls=%fused_computation.7 | convolution fusion | flops 151830528 | bytes 1705728 | tf_op jit(solution)/shard_map/dot_general | solution.py:148
  132.2 18.0 %reduce-window.6 = s32[64,8,128]{2,1,0:T(8,128)S(1)} reduce-window(s32[64,8,128]{2,1,0:T(8,128)S(1)} %fusion.41, s32[]{:T(128)} %constant.71.clone.1), window={size=1x1x128 pad=0_0x0_0x127_0}, to_apply=%region_6.7 | reduce-window | flops 8323072 | bytes 524292 | tf_op jit(solution)/shard_map/reduce-window
  150.8 4.5 %gather_fusion.1 = s32[1024]{0:T(1024)S(1)} fusion(s32[1024]{0:T(1024)S(1)} %fusion.37, s32[1024]{0:T(1024)S(1)} %fusion.81), kind=kCustom, calls=%fused_computation.clone | custom fusion | bytes 12288 | tf_op jit(solution)/shard_map/jit(_take)/gather | solution.py:163
  155.4 0.8 convolution_convert_fusion.12
  156.2 1.7 convolution_convert_fusion.10
  157.8 0.7 convolution_convert_fusion.9
  158.6 45.9 %all-reduce.3.cloned.1.call-done = bf16[256,1536]{1,0:T(8,128)(2,1)} async-done(((bf16[256,1536]{1,0:T(8,128)(2,1)}), bf16[256,1536]{1,0:T(8,128)(2,1)}) %all-reduce.3.cloned.1.call-update) | async-done | bytes 786448 | tf_op jit(solution)/shard_map/psum | solution.py:149
  204.5 1.5 fusion.3
  206.1 0.7 copy.103
  206.8 1.3 convolution_convert_fusion.3
  208.2 3.7 %fusion.10 = bf16[2,8,192,128]{3,1,2,0:T(8,128)(2,1)S(1)} fusion(bf16[16,64]{1,0:T(8,128)(2,1)S(1)} %convolution_convert_fusion.12, bf16[8,8,192,128]{3,2,1,0:T(8,128)(2,1)} %bitcast.34), kind=kOutput, calls=%fused_computation.22 | convolution fusion | flops 50724864 | bytes 3934208 | tf_op jit(solution)/shard_map/dot_general | solution.py:198
  211.8 1.0 copy.116
  (101 shorter events, 4.6 us)
Async XLA Ops:
  7.2 199.7 %copy-start = (bf16[1536,403]{0,1:T(8,128)(2,1)S(1)}, bf16[1536,403]{0,1:T(8,128)(2,1)}, u32[]{:S(2)}) copy-start(bf16[1536,403]{0,1:T(8,128)(2,1)} %param.42) | copy-start | bytes 3714052
  7.2 3.7 %copy-start.1 = (s32[1024]{0:T(1024)S(1)}, s32[1024]{0:T(1024)}, u32[]{:S(2)}) copy-start(s32[1024]{0:T(1024)} %param.45) | copy-start | bytes 12292
  10.9 4.6 %copy-start.12 = (s32[1024]{0:T(1024)S(1)}, s32[1024]{0:T(1024)}, u32[]{:S(2)}) copy-start(s32[1024]{0:T(1024)} %param.43) | copy-start | bytes 12292
  10.9 5.3 %copy-start.10 = (bf16[16,3,192]{2,0,1:T(8,128)(2,1)S(1)}, bf16[16,3,192]{2,0,1:T(8,128)(2,1)}, u32[]{:S(2)}) copy-start(bf16[16,3,192]{2,0,1:T(8,128)(2,1)} %param.26) | copy-start | bytes 55300
  10.9 5.3 %copy-start.7 = (bf16[256,192]{0,1:T(8,128)(2,1)S(1)}, bf16[256,192]{0,1:T(8,128)(2,1)}, u32[]{:S(2)}) copy-start(bf16[256,192]{0,1:T(8,128)(2,1)} %param.24) | copy-start | bytes 294916
  16.1 52.2 %copy-start.15 = (s32[16]{0:T(128)}, s32[16]{0:T(128)S(1)}, u32[]{:S(2)}) copy-start(s32[16]{0:T(128)S(1)} %dynamic_slice.10) | copy-start | bytes 196
  16.2 14.3 %copy-start.22 = (f32[1536]{0:T(1024)S(1)}, f32[1536]{0:T(1024)}, u32[]{:S(2)}) copy-start(f32[1536]{0:T(1024)} %param.28) | copy-start | bytes 18436
  30.5 20.7 %copy-start.25 = (f32[3]{0:T(128)S(1)}, f32[3]{0:T(128)}, u32[]{:S(2)}) copy-start(f32[3]{0:T(128)} %param.33) | copy-start | bytes 40
  30.5 20.7 %copy-start.13 = (bf16[4,192]{1,0:T(4,128)(2,1)S(1)}, bf16[4,192]{1,0:T(4,128)(2,1)}, u32[]{:S(2)}) copy-start(bf16[4,192]{1,0:T(4,128)(2,1)} %param.34) | copy-start | bytes 4612
  30.5 20.7 %copy-start.14 = (bf16[4,256]{1,0:T(4,128)(2,1)S(1)}, bf16[4,256]{1,0:T(4,128)(2,1)}, u32[]{:S(2)}) copy-start(bf16[4,256]{1,0:T(4,128)(2,1)} %param.36) | copy-start | bytes 6148
  30.5 21.4 %copy-start.11 = (bf16[16,3,256]{2,0,1:T(8,128)(2,1)S(1)}, bf16[16,3,256]{2,0,1:T(8,128)(2,1)}, u32[]{:S(2)}) copy-start(bf16[16,3,256]{2,0,1:T(8,128)(2,1)} %param.27) | copy-start | bytes 73732
  30.5 21.4 %copy-start.21 = (bf16[1536,3]{0,1:T(4,128)(2,1)S(1)}, bf16[1536,3]{0,1:T(4,128)(2,1)}, u32[]{:S(2)}) copy-start(bf16[1536,3]{0,1:T(4,128)(2,1)} %param.31) | copy-start | bytes 27652
  32.5 0.7 copy-start.6
  32.5 19.8 %copy-start.20 = (bf16[1536,32]{0,1:T(8,128)(2,1)S(1)}, bf16[1536,32]{0,1:T(8,128)(2,1)}, u32[]{:S(2)}) copy-start(bf16[1536,32]{0,1:T(8,128)(2,1)} %param.30) | copy-start | bytes 294916
  34.4 40.8 %all-to-all-start.1 = ((bf16[64,3,192]{2,1,0:T(4,128)(2,1)}), bf16[64,3,192]{2,1,0:T(4,128)(2,1)}, u32[]{:S(2)}, u32[]{:S(2)}) async-start(bf16[64,3,192]{2,1,0:T(4,128)(2,1)} %copy.98), calls=%async_computation.1 | async-start | bytes 262144 | tf_op jit(solution)/shard_map/all_to_all | solution.py:183
  51.0 1.8 copy-start.19
  52.3 17.1 %copy-start.17 = (f32[192]{0:T(256)S(1)}, f32[192]{0:T(256)}, u32[]{:S(2)}) copy-start(f32[192]{0:T(256)} %param.35) | copy-start | bytes 2308
  68.0 0.7 copy-start.5
  69.4 18.5 %copy-start.2 = (bf16[16,3,64,128]{3,2,1,0:T(8,128)(2,1)S(1)}, bf16[16,3,64,128]{3,2,1,0:T(8,128)(2,1)}, u32[]{:S(2)}) copy-start(bf16[16,3,64,128]{3,2,1,0:T(8,128)(2,1)} %param.25) | copy-start | bytes 2359300
  71.5 2.2 %copy-start.3 = (f32[16,16,3,64]{3,2,1,0:T(4,128)}, f32[16,16,3,64]{3,2,1,0:T(4,128)S(1)}, u32[]{:S(2)}) copy-start(f32[16,16,3,64]{3,2,1,0:T(4,128)S(1)} %reshape.238) | copy-start | bytes 589828
  75.2 23.6 %all-to-all-start.2 = ((bf16[64,3,256]{2,1,0:T(4,128)(2,1)}), bf16[64,3,256]{2,1,0:T(4,128)(2,1)S(1)}, u32[]{:S(2)}, u32[]{:S(2)}) async-start(bf16[64,3,256]{2,1,0:T(4,128)(2,1)} %copy.101), calls=%async_computation.2 | async-start | bytes 262144 | tf_op jit(solution)/shard_map/all_to_all | solution.py:184
  98.8 109.4 %all-to-all-start = ((bf16[64,3,64,128]{3,2,1,0:T(8,128)(2,1)}), bf16[64,3,64,128]{3,2,1,0:T(8,128)(2,1)}, u32[]{:S(2)}, u32[]{:S(2)}) async-start(bf16[64,3,64,128]{3,2,1,0:T(8,128)(2,1)} %bitcast.87), calls=%async_computation | async-start | bytes 6291456 | tf_op jit(solution)/shard_map/all_to_all | solution.py:182
  109.0 3.8 %copy-start.26 = (f32[3]{0:T(128)S(1)}, f32[3]{0:T(128)}, u32[]{:S(2)}) copy-start(f32[3]{0:T(128)} %param.38) | copy-start | bytes 40
  109.1 95.4 %all-reduce.3.cloned.1.call-start = ((), (), s32[]{:S(2)}) async-start(), calls=%async_computation.3 | async-start | bytes 1572864 | tf_op jit(solution)/shard_map/psum | solution.py:149
  110.7 2.1 copy-start.4
  110.7 2.1 copy-start.8
  110.7 2.1 copy-start.9
  112.9 16.8 %copy-start.24 = (f32[192]{0:T(256)S(1)}, f32[192]{0:T(256)}, u32[]{:S(2)}) copy-start(f32[192]{0:T(256)} %param.39) | copy-start | bytes 2308
  150.8 4.6 %copy-start.16 = (pred[1024]{0:T(1024)(128)(4,1)S(1)}, pred[1024]{0:T(1024)(128)(4,1)}, u32[]{:S(2)}) copy-start(pred[1024]{0:T(1024)(128)(4,1)} %get-tuple-element.28) | copy-start | bytes 3076
  150.8 4.6 %copy-start.18 = (pred[1024]{0:T(1024)(128)(4,1)S(1)}, pred[1024]{0:T(1024)(128)(4,1)}, u32[]{:S(2)}) copy-start(pred[1024]{0:T(1024)(128)(4,1)} %get-tuple-element.26) | copy-start | bytes 3076
  156.2 50.7 %copy-start.23 = (f32[1536]{0:T(1024)S(1)}, f32[1536]{0:T(1024)}, u32[]{:S(2)}) copy-start(f32[1536]{0:T(1024)} %param.41) | copy-start | bytes 18436
Sparse Core Ops, SparseCore 0:
  132.2 72.1 all-reduce.2
where the time goes:
time: 220 us
  waiting for transfers between devices  48.7 us (22%)
  blocking collectives  41 us (19%)
  starting transfers between devices  39.6 us (18%)
  other arithmetic  30.4 us (14%)
  local copies, waits for them, and re-layouts  22.8 us (10%)
  matrix products  22.6 us (10%)
  between operations  14.6 us (7%)
    psum x1, waiting for transfers between devices, local(): lax.psum(partial_sum.astype(jnp.bfloat16), 'narrow').astype(jnp.float32)  45.9 us
    another operation x3, other arithmetic  18.2 us
    all_to_all x1, starting transfers between devices, local(): lax.all_to_all(inner_bucket, 'wide', split_axis=0, concat_axis=0, tiled=T...  16.6 us
    psum x1, blocking collectives, local(): squares = lax.psum(jnp.sum(gated * gated, axis=1, keepdims=True), 'narrow')  14.5 us
    all_gather x1, blocking collectives, local(): full_rows = lax.all_gather(hidden, 'narrow', axis=1, tiled=True)  13.7 us
    all_gather x1, blocking collectives, local(): shared_in = lax.all_gather(shared_piece, 'narrow', axis=1, tiled=True)  12.7 us
    all_to_all x1, starting transfers between devices, local(): lax.all_to_all(shared_bucket, 'wide', split_axis=0, concat_axis=0, tiled=...  12.7 us
    all_to_all x1, starting transfers between devices, local(): lax.all_to_all(state_bucket, 'wide', split_axis=0, concat_axis=0, tiled=T...  10.3 us
  transfers between devices with their start and end apart: 4, of which 2 were waited for; matrix products, arithmetic and copies ran while one was open for 26% of the time, Pallas kernels for 0%

commit v1 on v0

--- a/solution.py
+++ b/solution.py
@@ -1,3 +1,4 @@
+import functools
 import jax
 import jax.numpy as jnp
 from jax import lax
@@ -5,6 +6,18 @@
 
 EPSILON = 1e-05
 HIGHEST = lax.Precision.HIGHEST
+
+
+def stocks_put(packet, row_dim, mesh_name):
+    return jnp.concatenate(
+        lax.all_to_all(
+            jnp.stack([packet for _ in range(lax.axis_size(mesh_name))]), mesh_name, 0, 0
+        ),
+        row_dim,
+    )
+
+
+convert_works_here = functools.partial(stocks_put, row_dim=1, mesh_name="narrow")
 
 
 def root_norm(values, gain):
@@ -103,7 +116,7 @@
     wide_index = lax.axis_index("wide")
     wide_count = lax.axis_size("wide")
     narrow_count = lax.axis_size("narrow")
-    full_rows = lax.all_gather(hidden, "narrow", axis=1, tiled=True)
+    full_rows = convert_works_here(hidden)
     normed_in = root_norm(full_rows, input_gain)
     tokens = full_rows.shape[0]
     requests = start_state.shape[0]

time: 220 us -> 239 us (1.086)
  the two profiles are of different devices: /device:TPU:24 before, /device:TPU:8 now
where the time goes in v1:
time: 239 us; the launch traced here: 238 us
  waiting for transfers between devices  87.4 us (37%)
  starting transfers between devices  35.6 us (15%)
  other arithmetic  27.2 us (11%)
  blocking collectives  26 us (11%)
  local copies, waits for them, and re-layouts  24.3 us (10%)
  matrix products  23.1 us (10%)
  between operations  14.6 us (6%)
    psum x1, waiting for transfers between devices, local(): lax.psum(partial_sum.astype(jnp.bfloat16), 'narrow').astype(jnp.float32)  67.9 us
    another operation x3, other arithmetic  18.2 us
    all_to_all x1, starting transfers between devices, local(): lax.all_to_all(inner_bucket, 'wide', split_axis=0, concat_axis=0, tiled=T...  16.8 us
    psum x1, blocking collectives, local(): squares = lax.psum(jnp.sum(gated * gated, axis=1, keepdims=True), 'narrow')  13.2 us
    all_gather x1, blocking collectives, local(): shared_in = lax.all_gather(shared_piece, 'narrow', axis=1, tiled=True)  12.7 us
    all_to_all x1, waiting for transfers between devices, local(): lax.all_to_all(inner_bucket, 'wide', split_axis=0, concat_axis=0, tiled=T...  8.64 us
    all_to_all x1, starting transfers between devices, local(): lax.all_to_all(state_bucket, 'wide', split_axis=0, concat_axis=0, tiled=T...  8.13 us
    all_to_all x1, starting transfers between devices, local(): lax.all_to_all(shared_bucket, 'wide', split_axis=0, concat_axis=0, tiled=...  6.36 us
  transfers between devices with their start and end apart: 5, of which 4 were waited for; matrix products, arithmetic and copies ran while one was open for 24% of the time, Pallas kernels for 0%

profile of v1, /device:TPU:8, one launch (start us, length us, event | category | flops | bytes accessed | tf_op | source)
XLA Modules:
  0.0 238.2 jit_solution(11876830229013089312)
XLA Ops:
  7.2 1.9 stack.2
  9.1 4.3 %all-to-all-start = ((bf16[8,256,192]{1,2,0:T(8,128)(2,1)}), bf16[8,256,192]{1,2,0:T(8,128)(2,1)S(1)}, u32[]{:S(2)}, u32[]{:S(2)}) async-start(bf16[8,256,192]{1,2,0:T(8,128)(2,1)} %stack.2), calls=%async_computation | async-start | bytes 1572864 | tf_op jit(solution)/shard_map/all_to_all | solution.py:13
  13.5 0.6 gather_fusion
  14.5 4.5 %gather_fusion.2 = s32[1024]{0:T(1024)S(1)} fusion(s32[1024]{0:T(1024)S(1)} %copy-done.1, s32[1024]{0:T(1024)S(1)} %fusion.77), kind=kCustom, calls=%fused_computation.1.clone | custom fusion | bytes 12288 | tf_op jit(solution)/shard_map/jit(_take)/gather | solution.py:175
  19.0 0.6 broadcast_compare_fusion
  19.9 0.6 slice_convert_fusion.7
  20.5 6.0 %all-to-all-done = bf16[8,256,192]{1,2,0:T(8,128)(2,1)S(1)} async-done(((bf16[8,256,192]{1,2,0:T(8,128)(2,1)}), bf16[8,256,192]{1,2,0:T(8,128)(2,1)S(1)}, u32[]{:S(2)}, u32[]{:S(2)}) %all-to-all-start) | async-done | bytes 786464 | tf_op jit(solution)/shard_map/all_to_all | solution.py:13
  26.6 0.2 multiply_reduce_fusion
  26.9 1.4 multiply_convert_fusion
  28.5 0.2 convolution_convert_fusion.11
  28.7 0.8 copy-done.8
  29.5 0.6 convolution_convert_fusion.4
  30.5 0.7 fusion.82
  31.7 0.8 copy.95
  32.6 12.7 %all_gather.3 = bf16[256,256]{0,1:T(8,128)(2,1)S(1)} all-gather(bf16[256,32]{0,1:T(8,128)(2,1)S(1)} %convolution_convert_fusion.11), channel_id=1, replica_groups=mesh['wide'=64,'narrow'=8] {'narrow'}, dimensions={1}, use_global_device_ids=true | all-gather | bytes 147456 | tf_op jit(solution)/shard_map/all_gather | solution.py:134
  45.7 0.3 convolution_convert_fusion.5
  46.0 0.7 copy.101
  47.0 0.3 convolution_convert_fusion.6
  47.3 0.7 copy.98
  48.1 16.8 %all-to-all-start.2 = ((bf16[64,3,192]{2,1,0:T(4,128)(2,1)}), bf16[64,3,192]{2,1,0:T(4,128)(2,1)}, u32[]{:S(2)}, u32[]{:S(2)}) async-start(bf16[64,3,192]{2,1,0:T(4,128)(2,1)} %copy.98), calls=%async_computation.2 | async-start | bytes 262144 | tf_op jit(solution)/shard_map/all_to_all | solution.py:196
  65.3 1.4 broadcast_multiply_fusion
  66.7 1.5 divide_multiply_fusion.1
  68.2 8.6 %all-to-all-done.2 = bf16[64,3,192]{2,1,0:T(4,128)(2,1)} async-done(((bf16[64,3,192]{2,1,0:T(4,128)(2,1)}), bf16[64,3,192]{2,1,0:T(4,128)(2,1)}, u32[]{:S(2)}, u32[]{:S(2)}) %all-to-all-start.2) | async-done | bytes 73760 | tf_op jit(solution)/shard_map/all_to_all | solution.py:196
  76.9 6.4 %all-to-all-start.3 = ((bf16[64,3,256]{2,1,0:T(4,128)(2,1)}), bf16[64,3,256]{2,1,0:T(4,128)(2,1)}, u32[]{:S(2)}, u32[]{:S(2)}) async-start(bf16[64,3,256]{2,1,0:T(4,128)(2,1)} %copy.101), calls=%async_computation.3 | async-start | bytes 262144 | tf_op jit(solution)/shard_map/all_to_all | solution.py:197
  83.3 2.8 %add_convert_fusion = bf16[16,3,64,128]{3,2,1,0:T(8,128)(2,1)S(1)} fusion(bf16[16,3,64,128]{3,2,1,0:T(8,128)(2,1)S(1)} %copy-done.5, f32[16,3]{1,0:T(8,128)S(1)} %copy.93, f32[16,16,3,64]{3,2,1,0:T(4,128)S(1)} %broadcast_multiply_fusion, f32[16,16,256]{2,1,0:T(8,128)S(1)} %divide_multiply_fusion.1), kind=kOutput, calls=%fused_computation.14 | convolution fusion | flops 77070336 | bytes 2236416 | tf_op jit(solution)/shard_map/rsh,rshp,rsn->rhpn/dot_general | solution.py:86
  86.1 1.8 fusion.2
  87.8 2.5 %copy.114 = bf16[8,8,192,128]{3,2,1,0:T(8,128)(2,1)} copy(bf16[8,8,192,128]{3,1,2,0:T(8,128)(2,1)S(1)} %fusion.2) | data formatting | bytes 6291456
  90.3 4.8 %all-to-all-done.3 = bf16[64,3,256]{2,1,0:T(4,128)(2,1)} async-done(((bf16[64,3,256]{2,1,0:T(4,128)(2,1)}), bf16[64,3,256]{2,1,0:T(4,128)(2,1)}, u32[]{:S(2)}, u32[]{:S(2)}) %all-to-all-start.3) | async-done | bytes 98336 | tf_op jit(solution)/shard_map/all_to_all | solution.py:197
  95.1 8.1 %all-to-all-start.1 = ((bf16[64,3,64,128]{3,2,1,0:T(8,128)(2,1)}), bf16[64,3,64,128]{3,2,1,0:T(8,128)(2,1)}, u32[]{:S(2)}, u32[]{:S(2)}) async-start(bf16[64,3,64,128]{3,2,1,0:T(8,128)(2,1)} %bitcast.94), calls=%async_computation.1 | async-start | bytes 6291456 | tf_op jit(solution)/shard_map/all_to_all | solution.py:195
  103.3 18.0 %reduce-window.6 = s32[64,8,128]{2,1,0:T(8,128)S(1)} reduce-window(s32[64,8,128]{2,1,0:T(8,128)S(1)} %fusion.37, s32[]{:T(128)} %constant.71.clone.1), window={size=1x1x128 pad=0_0x0_0x127_0}, to_apply=%region_6.7 | reduce-window | flops 8323072 | bytes 524292 | tf_op jit(solution)/shard_map/reduce-window
  122.0 4.5 %gather_fusion.1 = s32[1024]{0:T(1024)S(1)} fusion(s32[1024]{0:T(1024)S(1)} %fusion.33, s32[1024]{0:T(1024)S(1)} %fusion.77), kind=kCustom, calls=%fused_computation.clone | custom fusion | bytes 12288 | tf_op jit(solution)/shard_map/jit(_take)/gather | solution.py:176
  126.6 0.8 convolution_convert_fusion.12
  127.6 1.6 copy.90
  129.4 0.3 fusion.55
  129.8 2.9 %convolution_multiply_fusion = f32[16,16,3,64]{3,1,2,0:T(8,128)S(1)} fusion(bf16[16,3,64,128]{3,2,1,0:T(8,128)(2,1)} %param.25, f32[16,16,3]{1,2,0:T(4,128)S(1)} %copy.82, f32[16,16,256]{2,1,0:T(8,128)S(1)} %divide_multiply_fusion.1), kind=kOutput, calls=%fused_computation.22 | convolution fusion | flops 75546624 | bytes 1146880 | tf_op jit(solution)/shard_map/rtn,rhpn->rthp/dot_general | solution.py:72
  132.7 0.6 fusion.10
  133.5 0.3 reshape.245
  134.0 13.2 %psum.14 = f32[256,1]{0,1:T(1,128)S(1)} all-reduce(f32[256,1]{0,1:T(1,128)S(1)} %bitcast.104), channel_id=1, replica_groups=mesh['wide'=64,'narrow'=8] {'narrow'}, use_global_device_ids=true, to_apply=%region_3.4 | all-reduce | flops 256 | bytes 2048 | tf_op jit(solution)/shard_map/psum | solution.py:157
  147.3 2.5 %convolution_convert_fusion.2 = bf16[256,1536]{1,0:T(8,128)(2,1)} fusion(bf16[192,1536]{1,0:T(8,128)(2,1)} %param.40, f32[192]{0:T(256)S(1)} %copy-done.27, f32[256]{0:T(256)S(1)} %bitcast.113, f32[256,192]{1,0:T(8,128)S(1)} %reshape.245, bf16[256,384]{1,0:T(8,128)(2,1)S(1)} %copy-done.10), kind=kOutput, calls=%fused_computation.7 | convolution fusion | flops 151830528 | bytes 1771520 | tf_op jit(solution)/shard_map/dot_general | solution.py:161
  149.8 1.6 convolution_convert_fusion.10
  151.4 1.6 convolution_convert_fusion.9
  153.1 67.9 %all-reduce.3.cloned.1.call-done = bf16[256,1536]{1,0:T(8,128)(2,1)} async-done(((bf16[256,1536]{1,0:T(8,128)(2,1)}), bf16[256,1536]{1,0:T(8,128)(2,1)}) %all-reduce.3.cloned.1.call-update) | async-done | bytes 786448 | tf_op jit(solution)/shard_map/psum | solution.py:162
  221.0 1.5 fusion.3
  222.5 0.9 copy-done.11
  223.4 0.7 copy.103
  224.2 2.4 %convolution_convert_fusion.3 = bf16[256,403]{0,1:T(8,128)(2,1)} fusion(bf16[1536,403]{0,1:T(8,128)(2,1)S(1)} %copy-done, bf16[256,1536]{1,0:T(8,128)(2,1)} %copy-done.11, f32[1536]{0:T(1024)S(1)} %copy-done.26, f32[256]{0:T(256)S(1)} %add_rsqrt_fusion), kind=kOutput, calls=%fused_computation.23 | convolution fusion | flops 318608128 | bytes 2237952 | tf_op jit(solution)/shard_map/dot_general | solution.py:168
  226.6 3.7 %fusion.6 = bf16[2,8,192,128]{3,1,2,0:T(8,128)(2,1)S(1)} fusion(bf16[16,64]{1,0:T(8,128)(2,1)S(1)} %convolution_convert_fusion.12, bf16[8,8,192,128]{3,2,1,0:T(8,128)(2,1)} %bitcast.37), kind=kOutput, calls=%fused_computation.18 | convolution fusion | flops 50724864 | bytes 3934208 | tf_op jit(solution)/shard_map/dot_general | solution.py:211
  230.3 1.0 copy.116
  (110 shorter events, 4.5 us)
Async XLA Ops:
  7.2 217.0 %copy-start = (bf16[1536,403]{0,1:T(8,128)(2,1)S(1)}, bf16[1536,403]{0,1:T(8,128)(2,1)}, u32[]{:S(2)}) copy-start(bf16[1536,403]{0,1:T(8,128)(2,1)} %param.42) | copy-start | bytes 3714052
  7.2 6.2 %copy-start.16 = (s32[1024]{0:T(1024)S(1)}, s32[1024]{0:T(1024)}, u32[]{:S(2)}) copy-start(s32[1024]{0:T(1024)} %param.43) | copy-start | bytes 12292
  7.2 6.3 %copy-start.2 = (s32[1024]{0:T(1024)S(1)}, s32[1024]{0:T(1024)}, u32[]{:S(2)}) copy-start(s32[1024]{0:T(1024)} %param.44) | copy-start | bytes 12292
  7.2 7.2 %copy-start.1 = (s32[1024]{0:T(1024)S(1)}, s32[1024]{0:T(1024)}, u32[]{:S(2)}) copy-start(s32[1024]{0:T(1024)} %param.45) | copy-start | bytes 12292
  9.1 17.5 %all-to-all-start = ((bf16[8,256,192]{1,2,0:T(8,128)(2,1)}), bf16[8,256,192]{1,2,0:T(8,128)(2,1)S(1)}, u32[]{:S(2)}, u32[]{:S(2)}) async-start(bf16[8,256,192]{1,2,0:T(8,128)(2,1)} %stack.2), calls=%async_computation | async-start | bytes 1572864 | tf_op jit(solution)/shard_map/all_to_all | solution.py:13
  14.4 5.2 %copy-start.28 = (f32[3]{0:T(128)S(1)}, f32[3]{0:T(128)}, u32[]{:S(2)}) copy-start(f32[3]{0:T(128)} %param.33) | copy-start | bytes 40
  14.4 5.4 %copy-start.14 = (bf16[16,3,192]{2,0,1:T(8,128)(2,1)S(1)}, bf16[16,3,192]{2,0,1:T(8,128)(2,1)}, u32[]{:S(2)}) copy-start(bf16[16,3,192]{2,0,1:T(8,128)(2,1)} %param.26) | copy-start | bytes 55300
  14.4 5.4 %copy-start.15 = (bf16[16,3,256]{2,0,1:T(8,128)(2,1)S(1)}, bf16[16,3,256]{2,0,1:T(8,128)(2,1)}, u32[]{:S(2)}) copy-start(bf16[16,3,256]{2,0,1:T(8,128)(2,1)} %param.27) | copy-start | bytes 73732
  14.4 5.4 %copy-start.19 = (bf16[4,192]{1,0:T(4,128)(2,1)S(1)}, bf16[4,192]{1,0:T(4,128)(2,1)}, u32[]{:S(2)}) copy-start(bf16[4,192]{1,0:T(4,128)(2,1)} %param.34) | copy-start | bytes 4612
  14.5 5.4 %copy-start.20 = (bf16[4,256]{1,0:T(4,128)(2,1)S(1)}, bf16[4,256]{1,0:T(4,128)(2,1)}, u32[]{:S(2)}) copy-start(bf16[4,256]{1,0:T(4,128)(2,1)} %param.36) | copy-start | bytes 6148
  14.5 12.4 %copy-start.18 = (f32[1536]{0:T(1024)S(1)}, f32[1536]{0:T(1024)}, u32[]{:S(2)}) copy-start(f32[1536]{0:T(1024)} %param.28) | copy-start | bytes 18436
  19.7 27.3 %copy-start.21 = (s32[16]{0:T(128)}, s32[16]{0:T(128)S(1)}, u32[]{:S(2)}) copy-start(s32[16]{0:T(128)S(1)} %dynamic_slice.10) | copy-start | bytes 196
  26.8 1.4 copy-start.17
  26.9 1.6 copy-start.13
  28.2 1.3 copy-start.8
  28.5 1.8 copy-start.25
  30.1 18.0 %copy-start.9 = (bf16[256,384]{1,0:T(8,128)(2,1)}, bf16[256,384]{1,0:T(8,128)(2,1)S(1)}, u32[]{:S(2)}) copy-start(bf16[256,384]{1,0:T(8,128)(2,1)S(1)} %convolution_convert_fusion.4) | copy-start | bytes 589828
  30.5 34.4 %copy-start.23 = (f32[192]{0:T(256)S(1)}, f32[192]{0:T(256)}, u32[]{:S(2)}) copy-start(f32[192]{0:T(256)} %param.35) | copy-start | bytes 2308
  45.4 2.7 %copy-start.12 = (bf16[256,256]{1,0:T(8,128)(2,1)}, bf16[256,256]{1,0:T(8,128)(2,1)S(1)}, u32[]{:S(2)}) copy-start(bf16[256,256]{1,0:T(8,128)(2,1)S(1)} %copy.79) | copy-start | bytes 393220
  48.1 28.8 %all-to-all-start.2 = ((bf16[64,3,192]{2,1,0:T(4,128)(2,1)}), bf16[64,3,192]{2,1,0:T(4,128)(2,1)}, u32[]{:S(2)}, u32[]{:S(2)}) async-start(bf16[64,3,192]{2,1,0:T(4,128)(2,1)} %copy.98), calls=%async_computation.2 | async-start | bytes 262144 | tf_op jit(solution)/shard_map/all_to_all | solution.py:196
  64.9 18.4 %copy-start.5 = (bf16[16,3,64,128]{3,2,1,0:T(8,128)(2,1)S(1)}, bf16[16,3,64,128]{3,2,1,0:T(8,128)(2,1)}, u32[]{:S(2)}) copy-start(bf16[16,3,64,128]{3,2,1,0:T(8,128)(2,1)} %param.25) | copy-start | bytes 2359300
  65.3 20.7 %copy-start.6 = (f32[16,16,3,64]{3,2,1,0:T(4,128)}, f32[16,16,3,64]{3,2,1,0:T(4,128)S(1)}, u32[]{:S(2)}) copy-start(f32[16,16,3,64]{3,2,1,0:T(4,128)S(1)} %reshape.244) | copy-start | bytes 589828
  76.9 18.2 %all-to-all-start.3 = ((bf16[64,3,256]{2,1,0:T(4,128)(2,1)}), bf16[64,3,256]{2,1,0:T(4,128)(2,1)}, u32[]{:S(2)}, u32[]{:S(2)}) async-start(bf16[64,3,256]{2,1,0:T(4,128)(2,1)} %copy.101), calls=%async_computation.3 | async-start | bytes 262144 | tf_op jit(solution)/shard_map/all_to_all | solution.py:197
  95.1 131.5 %all-to-all-start.1 = ((bf16[64,3,64,128]{3,2,1,0:T(8,128)(2,1)}), bf16[64,3,64,128]{3,2,1,0:T(8,128)(2,1)}, u32[]{:S(2)}, u32[]{:S(2)}) async-start(bf16[64,3,64,128]{3,2,1,0:T(8,128)(2,1)} %bitcast.94), calls=%async_computation.1 | async-start | bytes 6291456 | tf_op jit(solution)/shard_map/all_to_all | solution.py:195
  103.3 117.7 %all-reduce.3.cloned.1.call-start = ((), (), s32[]{:S(2)}) async-start(), calls=%async_computation.4 | async-start | bytes 1572864 | tf_op jit(solution)/shard_map/psum | solution.py:162
  122.0 4.6 %copy-start.22 = (pred[1024]{0:T(1024)(128)(4,1)S(1)}, pred[1024]{0:T(1024)(128)(4,1)}, u32[]{:S(2)}) copy-start(pred[1024]{0:T(1024)(128)(4,1)} %get-tuple-element.28) | copy-start | bytes 3076
  122.0 4.6 %copy-start.24 = (pred[1024]{0:T(1024)(128)(4,1)S(1)}, pred[1024]{0:T(1024)(128)(4,1)}, u32[]{:S(2)}) copy-start(pred[1024]{0:T(1024)(128)(4,1)} %get-tuple-element.26) | copy-start | bytes 3076
  122.0 5.6 %copy-start.3 = (f32[8,256,192]{1,2,0:T(8,128)S(1)}, f32[8,256,192]{1,2,0:T(8,128)}, u32[]{:S(2)}) copy-start(f32[8,256,192]{1,2,0:T(8,128)} %get-tuple-element.34) | copy-start | bytes 4718596
  129.2 3.4 %copy-start.7 = (f32[16,16,3,64]{3,2,1,0:T(4,128)S(1)}, f32[16,16,3,64]{3,2,1,0:T(4,128)}, u32[]{:S(2)}) copy-start(f32[16,16,3,64]{3,2,1,0:T(4,128)} %copy-done.6) | copy-start | bytes 589828
  129.2 3.4 %copy-start.29 = (f32[3]{0:T(128)S(1)}, f32[3]{0:T(128)}, u32[]{:S(2)}) copy-start(f32[3]{0:T(128)} %param.38) | copy-start | bytes 40
  132.7 1.2 copy-start.10
  132.7 14.6 %copy-start.27 = (f32[192]{0:T(256)S(1)}, f32[192]{0:T(256)}, u32[]{:S(2)}) copy-start(f32[192]{0:T(256)} %param.39) | copy-start | bytes 2308
  147.3 73.7 %copy-start.4 = (f32[256,1536]{1,0:T(8,128)S(1)}, f32[256,1536]{1,0:T(8,128)}, u32[]{:S(2)}) copy-start(f32[256,1536]{1,0:T(8,128)} %copy.90) | copy-start | bytes 4718596
  153.1 71.1 %copy-start.26 = (f32[1536]{0:T(1024)S(1)}, f32[1536]{0:T(1024)}, u32[]{:S(2)}) copy-start(f32[1536]{0:T(1024)} %param.41) | copy-start | bytes 18436
  222.5 0.9 copy-start.11
Sparse Core Ops, SparseCore 0:
  149.9 71.0 all-reduce.2
